TPU v7x, 32 devices: a whole 2x2x4 slice. The times are simulated.
32 devices in a mesh: dom: 16 (over z, x, core), col: 2 (over y).
Axes of the slice: x: 2, y: 2, z: 4, core: 2. Of those that a mesh axis runs over, the one named last changes fastest.
Arguments:
- feats: bfloat16 [8192, 256], P('dom', 'col'), may hold values from -6 to 6
- w_first: bfloat16 [256, 256], replicated, may hold values from -0.375 to 0.375
- w_second: bfloat16 [256, 256], replicated, may hold values from -0.375 to 0.375
- block_cols: int32 [64, 32], P('dom'), may hold values from 0 to 63, as said below
- block_count: int32 [64], P('dom'), may hold values from 1 to 32
- block_vals: bfloat16 [64, 32, 128, 128], P('dom', 'col'), may hold values from -0.125 to 0.125
- cotangent: bfloat16 [8192, 256], P('dom', 'col'), may hold values from -6 to 6
Outputs:
- output: float32 [8192, 256], P('dom', 'col')
- grad_first: float32 [256, 256], P(None, 'col')
- grad_second: float32 [256, 256], P(None, 'col')
Inputs may be any that keep to these rules, and one draw needn't show every extreme that they name: Each row of block_cols names 32 different column blocks.
All inputs are finite; a program needn't handle non-finite values.
Results may differ from a plain program's by a relative error of at most 0.019.
Values may be sent and summed in bfloat16 or wider, within the bound.
No kernel may reach another device: no remote copies, remote signals or barrier semaphores. Data moves between devices by JAX's collectives and lax.ppermute only.
A program may use at most 64 MiB of HBM per device.

v0:
```python
import jax
import jax.numpy as jnp
from jax import lax
from jax.sharding import PartitionSpec as P

BLK = 128


def silu_slope(value):
    sig = jax.nn.sigmoid(value)
    return sig + value * sig * (1.0 - sig)


def forward_fold(prod, cols, vals):
    rows, width = prod.shape
    piece = lax.all_gather(prod, "dom", axis=0, tiled=True)
    count_blocks = piece.shape[0] // BLK
    hit = (cols >= 0) & (cols < count_blocks)
    picked = piece.reshape(count_blocks, BLK, width)[jnp.clip(cols, 0, count_blocks - 1)]
    picked = jnp.where(hit[:, :, None, None], picked, jnp.zeros((), picked.dtype))
    contrib = jnp.einsum("rkij,rkjf->rif", vals, picked, preferred_element_type=jnp.float32)
    return contrib.reshape(rows, width)


def backward_scatter(grad, cols, vals):
    rows, width = grad.shape
    nblocks = rows // BLK
    products = jnp.einsum(
        "rkij,rif->rkjf",
        vals,
        grad.reshape(nblocks, BLK, width),
        preferred_element_type=jnp.float32,
    )
    count = rows * lax.axis_size("dom")
    count_blocks = count // BLK
    onehot = (cols[:, :, None] == jnp.arange(count_blocks)[None, None, :]).astype(jnp.float32)
    summed = jnp.einsum("rkp,rkjf->pjf", onehot, products, precision=lax.Precision.HIGHEST)
    return lax.psum_scatter(summed.reshape(count, width), "dom", scatter_dimension=0, tiled=True)


def body(feats, w_first, w_second, block_cols, block_count, block_vals, cotangent):
    col_index = lax.axis_index("col")
    rows, narrow = feats.shape

    def widen(value):
        return lax.all_gather(value, "col", axis=1, tiled=True)

    def weight_grad(full, back):
        return lax.psum(
            jnp.dot(full.T, back, preferred_element_type=jnp.float32).astype(jnp.bfloat16), "dom"
        ).astype(jnp.float32)

    all_vals = lax.all_gather(block_vals, "col", axis=1, tiled=True)
    slot_ids = jnp.arange(all_vals.shape[1])
    usable = slot_ids[None, :] < block_count[:, None]
    vals = jnp.where(usable[:, :, None, None], all_vals, jnp.zeros((), all_vals.dtype))

    def project(full, weight):
        weight_cols = lax.dynamic_slice_in_dim(weight, col_index * narrow, narrow, 1)
        return jnp.dot(full, weight_cols, preferred_element_type=jnp.float32).astype(jnp.bfloat16)

    def aggregate(prod):
        return forward_fold(prod, block_cols, vals)

    def transpose(grad):
        return backward_scatter(grad, block_cols, vals)

    full_input = widen(feats)
    first = aggregate(project(full_input, w_first))
    hidden = (first * jax.nn.sigmoid(first)).astype(jnp.bfloat16)
    full_hidden = widen(hidden)
    output = aggregate(project(full_hidden, w_second))
    back_second = transpose(cotangent).astype(jnp.bfloat16)
    grad_second = weight_grad(full_hidden, back_second)
    second_cols = lax.dynamic_slice_in_dim(w_second, col_index * narrow, narrow, 1)
    partial_hidden = jnp.dot(back_second, second_cols.T, preferred_element_type=jnp.float32)
    hidden_grad = lax.psum_scatter(partial_hidden, "col", scatter_dimension=1, tiled=True)
    act_grad = (hidden_grad * silu_slope(first)).astype(jnp.bfloat16)
    back_first = transpose(act_grad).astype(jnp.bfloat16)
    grad_first = weight_grad(full_input, back_first)
    return (output, grad_first, grad_second)


def solution(mesh):
    in_specs = (
        P("dom", "col"),
        P(),
        P(),
        P("dom", None),
        P("dom"),
        P("dom", "col", None, None),
        P("dom", "col"),
    )
    out_specs = (P("dom", "col"), P(None, "col"), P(None, "col"))
    return jax.shard_map(body, mesh=mesh, in_specs=in_specs, out_specs=out_specs, check_vma=False)
```

profile of v0, /device:TPU:8, one launch (start us, length us, event | category | flops | bytes accessed | tf_op | source)
XLA Modules:
  0.0 452.0 jit_solution(4109258928189561779)
XLA Ops:
  8.7 58.8 %all-gather.4.cloned.1.call-done = bf16[4,32,128,128]{3,2,1,0:T(8,128)(2,1)} async-done(((bf16[4,16,128,128]{3,2,1,0:T(8,128)(2,1)}), bf16[4,32,128,128]{3,2,1,0:T(8,128)(2,1)}) %all-gather.4.cloned.1.call-update) | async-done | bytes 4194320 | tf_op jit(solution)/shard_map/all_gather | solution.py:53
  67.4 4.5 broadcast_select_fusion
  71.9 7.9 %copy.18 = bf16[4,32,128,128]{2,1,0,3:T(8,128)(2,1)} copy(bf16[4,32,128,128]{3,2,1,0:T(8,128)(2,1)} %broadcast_select_fusion) | data formatting | bytes 8388608 | tf_op jit(solution)/shard_map/jit(_where)/select_n | solution.py:56
  79.9 3.4 fusion.31
  83.3 3.9 convolution_bitcast_fusion.1
  87.3 4.4 copy.13
  92.6 5.8 %all_gather.16 = bf16[512,256]{1,0:T(8,128)(2,1)S(1)} all-gather(bf16[512,128]{1,0:T(8,128)(2,1)S(1)} %copy-done.2), channel_id=1, replica_groups=mesh['dom'=16,'col'=2] {'col'}, dimensions={1}, use_global_device_ids=true | all-gather | bytes 393216 | tf_op jit(solution)/shard_map/all_gather | solution.py:46
  99.3 64.6 %reduce-scatter.4.cloned.1.call-done = f32[512,128]{1,0:T(8,128)} async-done(((f32[8192,128]{1,0:T(8,128)}), f32[512,128]{1,0:T(8,128)}) %reduce-scatter.4.cloned.1.call-update) | async-done | bytes 262160 | tf_op jit(solution)/shard_map/reduce_scatter | solution.py:38
  163.9 2.0 fusion.16
  166.1 40.7 %all-gather.6.cloned.1.call-done = bf16[8192,128]{0,1:T(8,128)(2,1)} async-done(((bf16[512,128]{0,1:T(8,128)(2,1)}), bf16[8192,128]{0,1:T(8,128)(2,1)}) %all-gather.6.cloned.1.call-update) | async-done | bytes 2097168 | tf_op jit(solution)/shard_map/all_gather | solution.py:16
  206.8 3.2 copy.21
  210.0 3.0 gather_fusion
  213.0 5.0 %fusion.2 = f32[4,128,128,1]{2,1,3,0:T(8,128)S(1)} fusion(bf16[4,32,128,128]{3,2,1,0:T(8,128)(2,1)} %broadcast_select_fusion, bf16[4,32,128,128]{3,2,1,0:T(8,128)(2,1)} %bitcast.68, pred[4,32]{1,0:T(4,128)(4,1)S(1)} %compare_and_fusion), kind=kOutput, calls=%fused_computation.4 | convolution fusion | flops 538968064 | bytes 8650880 | tf_op jit(solution)/shard_map/rkij,rkjf->rif/dot_general | solution.py:21
  218.0 5.3 %reduce-scatter.6.cloned.1.call-done = f32[512,128]{1,0:T(8,128)} async-done(((f32[512,256]{1,0:T(8,128)}), f32[512,128]{1,0:T(8,128)}) %reduce-scatter.6.cloned.1.call-update) | async-done | bytes 262160 | tf_op jit(solution)/shard_map/reduce_scatter | solution.py:77
  224.4 5.8 %all_gather.18 = bf16[512,256]{1,0:T(8,128)(2,1)S(1)} all-gather(bf16[512,128]{1,0:T(8,128)(2,1)S(1)} %get-tuple-element.12), channel_id=1, replica_groups=mesh['dom'=16,'col'=2] {'col'}, dimensions={1}, use_global_device_ids=true | all-gather | bytes 393216 | tf_op jit(solution)/shard_map/all_gather | solution.py:46
  231.3 3.4 fusion.32
  234.8 3.9 convolution_bitcast_fusion
  238.7 4.4 copy.14
  245.0 26.6 %all-gather.8.cloned.1.call-done = bf16[8192,128]{1,0:T(8,128)(2,1)} async-done(((bf16[512,128]{1,0:T(8,128)(2,1)}), bf16[8192,128]{1,0:T(8,128)(2,1)}) %all-gather.8.cloned.1.call-update) | async-done | bytes 2097168 | tf_op jit(solution)/shard_map/all_gather | solution.py:16
  271.6 4.7 %gather_fusion.1 = bf16[128,128,128]{2,1,0:T(8,128)(2,1)} fusion(bf16[64,128,128]{2,1,0:T(8,128)(2,1)} %bitcast.66, s32[1024]{0:T(1024)S(1)} %pad_clamp_fusion), kind=kCustom, calls=%fused_computation.1 | custom fusion | bytes 8389120 | tf_op jit(solution)/shard_map/gather | solution.py:19
  276.2 71.0 %reduce-scatter.8.cloned.1.call-done = f32[512,128]{1,0:T(8,128)} async-done(((f32[8192,128]{1,0:T(8,128)}), f32[512,128]{1,0:T(8,128)}) %reduce-scatter.8.cloned.1.call-update) | async-done | bytes 262160 | tf_op jit(solution)/shard_map/reduce_scatter | solution.py:38
  347.3 1.8 fusion.9
  349.1 5.5 %fusion = f32[4,128,128,1]{2,1,3,0:T(8,128)} fusion(bf16[4,32,128,128]{3,2,1,0:T(8,128)(2,1)} %broadcast_select_fusion, bf16[4,32,128,128]{3,2,1,0:T(8,128)(2,1)} %bitcast.67, pred[4,32]{1,0:T(4,128)(4,1)S(1)} %compare_and_fusion), kind=kOutput, calls=%fused_computation.2 | convolution fusion | flops 538968064 | bytes 8650880 | tf_op jit(solution)/shard_map/rkij,rkjf->rif/dot_general | solution.py:21
  354.6 87.5 %all-reduce.3.cloned.1.call-done = (bf16[256,128]{0,1:T(8,128)(2,1)}, bf16[256,128]{1,0:T(8,128)(2,1)}) async-done(((bf16[256,128]{0,1:T(8,128)(2,1)}, bf16[256,128]{1,0:T(8,128)(2,1)}), (bf16[256,128]{0,1:T(8,128)(2,1)}, bf16[256,128]{1,0:T(8,128)(2,1)})) %all-reduce.3.cloned.1.call-update) | async-done | bytes 131088 | tf_op jit(solution)/shard_map/psum | solution.py:49
  (37 shorter events, 10.6 us)
Async XLA Ops:
  7.2 72.7 %copy-start = (bf16[512,128]{1,0:T(8,128)(2,1)S(1)}, bf16[512,128]{1,0:T(8,128)(2,1)}, u32[]{:S(2)}) copy-start(bf16[512,128]{1,0:T(8,128)(2,1)} %param.13) | copy-start | bytes 393220
  7.2 60.3 %all-gather.4.cloned.1.call-start = ((), (), s32[]{:S(2)}) async-start(), calls=%async_computation.3 | async-start | bytes 6291456 | tf_op jit(solution)/shard_map/all_gather | solution.py:53
  7.9 156.0 %reduce-scatter.4.cloned.1.call-start = ((), (), s32[]{:S(2)}) async-start(), calls=%async_computation.6 | async-start | bytes 4456448 | tf_op jit(solution)/shard_map/reduce_scatter | solution.py:38
  79.9 3.4 copy-start.5
  91.7 0.9 copy-start.2
  91.7 6.7 %copy-start.4 = (bf16[256,256]{1,0:T(8,128)(2,1)S(1)}, bf16[256,256]{1,0:T(8,128)(2,1)}, u32[]{:S(2)}) copy-start(bf16[256,256]{1,0:T(8,128)(2,1)} %param.8) | copy-start | bytes 393220
  91.7 72.2 %copy-start.3 = (bf16[256,256]{1,0:T(8,128)(2,1)S(1)}, bf16[256,256]{1,0:T(8,128)(2,1)}, u32[]{:S(2)}) copy-start(bf16[256,256]{1,0:T(8,128)(2,1)} %param.9) | copy-start | bytes 393220
  91.7 115.1 %all-gather.6.cloned.1.call-start = ((), (), s32[]{:S(2)}) async-start(), calls=%async_computation.4 | async-start | bytes 2228224 | tf_op jit(solution)/shard_map/all_gather | solution.py:16
  99.3 124.0 %reduce-scatter.6.cloned.1.call-start = ((), (), s32[]{:S(2)}) async-start(), calls=%async_computation.7 | async-start | bytes 786432 | tf_op jit(solution)/shard_map/reduce_scatter | solution.py:77
  165.9 105.6 %all-gather.8.cloned.1.call-start = ((), (), s32[]{:S(2)}) async-start(), calls=%async_computation.5 | async-start | bytes 2228224 | tf_op jit(solution)/shard_map/all_gather | solution.py:16
  231.1 116.2 %reduce-scatter.8.cloned.1.call-start = ((), (), s32[]{:S(2)}) async-start(), calls=%async_computation.8 | async-start | bytes 4456448 | tf_op jit(solution)/shard_map/reduce_scatter | solution.py:38
  243.1 0.9 copy-start.1
  243.1 199.0 %all-reduce.3.cloned.1.call-start = ((), (), s32[]{:S(2)}) async-start(), calls=%async_computation.9 | async-start | bytes 262144 | tf_op jit(solution)/shard_map/psum | solution.py:49
Sparse Core Ops, SparseCore 0:
  9.5 57.8 all-gather.3
  91.8 72.0 reduce-scatter.3
  166.7 40.0 all-gather.5
  208.8 14.4 reduce-scatter.5
  231.2 40.2 all-gather.7
  275.3 71.9 reduce-scatter.7
  351.4 90.6 all-reduce.2
where the time goes:
time: 453 us; the launch traced here: 452 us
  waiting for transfers between devices  355 us (78%)
  matrix products  31.6 us (7%)
  local copies, waits for them, and re-layouts  31 us (7%)
  between operations  14.2 us (3%)
  blocking collectives  11.6 us (3%)
  other arithmetic  7.83 us (2%)
    reduce_scatter x2, waiting for transfers between devices, backward_scatter(): lax.psum_scatter(summed.reshape(count, width), 'dom', scatter_dimension=0...  136 us
    psum x1, waiting for transfers between devices, weight_grad(): lax.psum(jnp.dot(full.T, back, preferred_element_type=jnp.float32).astype...  87.5 us
    all_gather x2, waiting for transfers between devices, forward_fold(): piece = lax.all_gather(prod, 'dom', axis=0, tiled=True)  67.3 us
    all_gather x1, waiting for transfers between devices, body(): all_vals = lax.all_gather(block_vals, 'col', axis=1, tiled=True)  58.8 us
    all_gather x2, blocking collectives, widen(): return lax.all_gather(value, 'col', axis=1, tiled=True)  11.6 us
    dot_general x2, matrix products, forward_fold(): jnp.einsum('rkij,rkjf->rif', vals, picked, preferred_element_type=jnp.flo...  10.4 us
  transfers between devices with their start and end apart: 7, of which 7 were waited for; matrix products, arithmetic and copies ran while one was open for 8% of the time, Pallas kernels for 0%

commit v1 on v0

--- a/solution.py
+++ b/solution.py
@@ -4,6 +4,19 @@
 from jax.sharding import PartitionSpec as P
 
 BLK = 128
+
+
+def ring_gather(array, axis, dim):
+    ways = lax.axis_size(axis)
+    up = [(d, (d + 1) % ways) for d in range(ways)]
+    down = [(d, (d - 1) % ways) for d in range(ways)]
+    earlier, later = ([array], [array])
+    for _ in range(ways // 2):
+        earlier.append(lax.ppermute(earlier[-1], axis, up))
+    for _ in range((ways - 1) // 2):
+        later.append(lax.ppermute(later[-1], axis, down))
+    line = jnp.concatenate([*earlier[::-1], *later[1:]], axis=dim)
+    return jnp.roll(line, (lax.axis_index(axis) - ways // 2) * array.shape[dim], axis=dim)
 
 
 def silu_slope(value):
@@ -13,7 +26,7 @@
 
 def forward_fold(prod, cols, vals):
     rows, width = prod.shape
-    piece = lax.all_gather(prod, "dom", axis=0, tiled=True)
+    piece = ring_gather(prod, "dom", 0)
     count_blocks = piece.shape[0] // BLK
     hit = (cols >= 0) & (cols < count_blocks)
     picked = piece.reshape(count_blocks, BLK, width)[jnp.clip(cols, 0, count_blocks - 1)]

time: 453 us -> 387 us (0.85)
  waiting for transfers between devices: 355 us -> 238 us
  starting transfers between devices: 0.47 us -> 40.5 us
  other arithmetic: 7.83 us -> 16.9 us
    reduce_scatter x2, waiting for transfers between devices: 136 us -> 29.1 us  [backward_scatter(): lax.psum_scatter(summed.reshape(count, width), 'dom', scatter_dimension=0...]
    all_gather x2 -> x0, waiting for transfers between devices: 67.3 us -> none  [forward_fold(): piece = lax.all_gather(prod, 'dom', axis=0, tiled=True)]
    ppermute x0 -> x30, waiting for transfers between devices: none -> 60.1 us  [the longest x16 50.4 us: ring_gather(): earlier.append(lax.ppermute(earlier[-1], axis, up))]
    ppermute x0 -> x30, starting transfers between devices: none -> 40.1 us  [the longest x14 39.7 us: ring_gather(): later.append(lax.ppermute(later[-1], axis, down))]
    concatenate x0 -> x2, other arithmetic: none -> 9.71 us  [ring_gather(): jnp.roll(line, (lax.axis_index(axis) - ways // 2) * array.shape[dim], axi...]
    unnamed x13 -> x59, local copies, waits for them, and re-layouts: 3.31 us -> 8.4 us
    reduce_scatter x1, waiting for transfers between devices: 5.31 us -> 0.46 us  [body(): lax.psum_scatter(partial_hidden, 'col', scatter_dimension=1, tiled=True)]
  transfers between devices with their start and end apart: 7 -> 35, of which waited for: 7 -> 28; matrix products, arithmetic and copies ran while one was open for 8% -> 10% of each run, Pallas kernels for 0% -> 0%
where the time goes in v1:
time: 387 us; the launch traced here: 386 us
  waiting for transfers between devices  238 us (61%)
  starting transfers between devices  40.5 us (10%)
  local copies, waits for them, and re-layouts  34.9 us (9%)
  matrix products  30.2 us (8%)
  other arithmetic  16.9 us (4%)
  between operations  14.2 us (4%)
  blocking collectives  11.6 us (3%)
    psum x1, waiting for transfers between devices, weight_grad(): lax.psum(jnp.dot(full.T, back, preferred_element_type=jnp.float32).astype...  87.8 us
    all_gather x1, waiting for transfers between devices, body(): all_vals = lax.all_gather(block_vals, 'col', axis=1, tiled=True)  59.4 us
    ppermute x16, waiting for transfers between devices, ring_gather(): earlier.append(lax.ppermute(earlier[-1], axis, up))  50.4 us
    ppermute x14, starting transfers between devices, ring_gather(): later.append(lax.ppermute(later[-1], axis, down))  39.7 us
    reduce_scatter x2, waiting for transfers between devices, backward_scatter(): lax.psum_scatter(summed.reshape(count, width), 'dom', scatter_dimension=0...  29.1 us
    all_gather x2, blocking collectives, widen(): return lax.all_gather(value, 'col', axis=1, tiled=True)  11.6 us
    dot_general x2, matrix products, forward_fold(): jnp.einsum('rkij,rkjf->rif', vals, picked, preferred_element_type=jnp.flo...  10.3 us
    concatenate x2, other arithmetic, ring_gather(): jnp.roll(line, (lax.axis_index(axis) - ways // 2) * array.shape[dim], axi...  9.71 us
  transfers between devices with their start and end apart: 35, of which 28 were waited for; matrix products, arithmetic and copies ran while one was open for 10% of the time, Pallas kernels for 0%

profile of v1, /device:TPU:8, one launch (start us, length us, event | category | flops | bytes accessed | tf_op | source)
XLA Modules:
  0.0 385.9 jit_solution(2174447159868408131)
XLA Ops:
  8.1 59.4 %all-gather.2.cloned.1.call-done = bf16[4,32,128,128]{3,2,1,0:T(8,128)(2,1)} async-done(((bf16[4,16,128,128]{3,2,1,0:T(8,128)(2,1)}), bf16[4,32,128,128]{3,2,1,0:T(8,128)(2,1)}) %all-gather.2.cloned.1.call-update) | async-done | bytes 4194320 | tf_op jit(solution)/shard_map/all_gather | solution.py:66
  67.5 4.5 %broadcast_select_fusion = bf16[4,32,128,128]{3,2,1,0:T(8,128)(2,1)} fusion(bf16[4,32,128,128]{3,2,1,0:T(8,128)(2,1)} %all-gather.2.cloned.1.call-done, pred[4,32]{1,0:T(4,128)(4,1)S(1)} %iota_compare_fusion.1), kind=kLoop, calls=%fused_computation.12 | loop fusion | flops 2097152 | bytes 8388736 | tf_op jit(solution)/shard_map/jit(_where)/select_n | solution.py:69
  72.0 8.0 %copy.17 = bf16[4,32,128,128]{2,1,0,3:T(8,128)(2,1)} copy(bf16[4,32,128,128]{3,2,1,0:T(8,128)(2,1)} %broadcast_select_fusion) | data formatting | bytes 8388608 | tf_op jit(solution)/shard_map/jit(_where)/select_n | solution.py:69
  79.9 3.4 fusion.33
  83.4 3.9 %convolution_bitcast_fusion.1 = f32[64,128,128]{2,0,1:T(8,128)S(1)} fusion(f32[4,32,128,128]{3,1,0,2:T(8,128)S(1)} %fusion.33, s32[4,32]{1,0:T(4,128)S(1)} %copy-done.12), kind=kOutput, calls=%fused_computation.14 | convolution fusion | flops 1610620928 | bytes 12583424 | tf_op jit(solution)/shard_map/rkp,rkjf->pjf/dot_general | solution.py:50
  87.3 4.5 %copy.16 = f32[64,128,128]{2,1,0:T(8,128)} copy(f32[64,128,128]{2,0,1:T(8,128)S(1)} %convolution_bitcast_fusion.1) | data formatting | bytes 8388608 | tf_op jit(solution)/shard_map/rkp,rkjf->pjf/dot_general | solution.py:50
  92.7 5.8 %all_gather.10 = bf16[512,256]{1,0:T(8,128)(2,1)S(1)} all-gather(bf16[512,128]{1,0:T(8,128)(2,1)S(1)} %copy-done.3), channel_id=1, replica_groups=mesh['dom'=16,'col'=2] {'col'}, dimensions={1}, use_global_device_ids=true | all-gather | bytes 393216 | tf_op jit(solution)/shard_map/all_gather | solution.py:59
  98.8 5.3 %collective-permute-done = bf16[512,128]{0,1:T(8,128)(2,1)S(1)} collective-permute-done((bf16[512,128]{0,1:T(8,128)(2,1)S(1)}, bf16[512,128]{0,1:T(8,128)(2,1)S(1)}, u32[]{:S(2)}, u32[]{:S(2)}) %collective-permute-start) | collective-permute-done | bytes 131104 | tf_op jit(solution)/shard_map/ppermute | solution.py:15
  122.9 5.3 %collective-permute-done.4 = bf16[512,128]{0,1:T(8,128)(2,1)S(1)} collective-permute-done((bf16[512,128]{0,1:T(8,128)(2,1)S(1)}, bf16[512,128]{0,1:T(8,128)(2,1)S(1)}, u32[]{:S(2)}, u32[]{:S(2)}) %collective-permute-start.4) | collective-permute-done | bytes 131104 | tf_op jit(solution)/shard_map/ppermute | solution.py:15
  134.9 3.3 collective-permute-start.13
  144.3 3.6 collective-permute-done.7
  153.6 18.4 %reduce-scatter.4.cloned.1.call-done = f32[512,128]{1,0:T(8,128)} async-done(((f32[8192,128]{1,0:T(8,128)}), f32[512,128]{1,0:T(8,128)}) %reduce-scatter.4.cloned.1.call-update) | async-done | bytes 262160 | tf_op jit(solution)/shard_map/reduce_scatter | solution.py:51
  183.0 4.8 %fusion.2 = f32[4,128,128,1]{2,1,3,0:T(8,128)S(1)} fusion(bf16[4,32,128,128]{3,2,1,0:T(8,128)(2,1)} %broadcast_select_fusion, bf16[4,32,128,128]{3,2,1,0:T(8,128)(2,1)} %bitcast.68, pred[4,32]{1,0:T(4,128)(4,1)S(1)} %compare_and_fusion), kind=kOutput, calls=%fused_computation.8 | convolution fusion | flops 538968064 | bytes 8650880 | tf_op jit(solution)/shard_map/rkij,rkjf->rif/dot_general | solution.py:34
  189.4 3.4 fusion.34
  192.8 3.9 %convolution_bitcast_fusion = f32[64,128,128]{2,0,1:T(8,128)S(1)} fusion(f32[4,32,128,128]{3,1,0,2:T(8,128)S(1)} %fusion.34, s32[4,32]{1,0:T(4,128)S(1)} %copy-done.12), kind=kOutput, calls=%fused_computation.13 | convolution fusion | flops 1610620928 | bytes 12583424 | tf_op jit(solution)/shard_map/rkp,rkjf->pjf/dot_general | solution.py:50
  196.8 4.5 %copy.18 = f32[64,128,128]{2,1,0:T(8,128)} copy(f32[64,128,128]{2,0,1:T(8,128)S(1)} %convolution_bitcast_fusion) | data formatting | bytes 8388608 | tf_op jit(solution)/shard_map/rkp,rkjf->pjf/dot_general | solution.py:50
  201.4 5.8 %all_gather.11 = bf16[512,256]{1,0:T(8,128)(2,1)S(1)} all-gather(bf16[512,128]{1,0:T(8,128)(2,1)S(1)} %get-tuple-element.16), channel_id=1, replica_groups=mesh['dom'=16,'col'=2] {'col'}, dimensions={1}, use_global_device_ids=true | all-gather | bytes 393216 | tf_op jit(solution)/shard_map/all_gather | solution.py:59
  207.5 5.3 %collective-permute-done.15 = bf16[512,128]{1,0:T(8,128)(2,1)S(1)} collective-permute-done((bf16[512,128]{1,0:T(8,128)(2,1)S(1)}, bf16[512,128]{1,0:T(8,128)(2,1)S(1)}, u32[]{:S(2)}, u32[]{:S(2)}) %collective-permute-start.15) | collective-permute-done | bytes 131104 | tf_op jit(solution)/shard_map/ppermute | solution.py:15
  231.6 5.3 %collective-permute-done.19 = bf16[512,128]{1,0:T(8,128)(2,1)S(1)} collective-permute-done((bf16[512,128]{1,0:T(8,128)(2,1)S(1)}, bf16[512,128]{1,0:T(8,128)(2,1)S(1)}, u32[]{:S(2)}, u32[]{:S(2)}) %collective-permute-start.19) | collective-permute-done | bytes 131104 | tf_op jit(solution)/shard_map/ppermute | solution.py:15
  256.5 3.4 collective-permute-done.29
  259.9 7.3 %fusion.6 = bf16[8192,128]{1,0:T(8,128)(2,1)S(1)} fusion(s32[]{:T(128)S(6)} %select_n.37, bf16[8192,128]{1,0:T(8,128)(2,1)S(1)} %constant_dynamic-update-slice_fusion.16), kind=kLoop, calls=%fused_computation.15 | loop fusion | flops 4194304 | bytes 4194308 | tf_op jit(solution)/shard_map/jit(_roll_dynamic)/concatenate | solution.py:19
  270.3 10.7 %reduce-scatter.8.cloned.1.call-done = f32[512,128]{1,0:T(8,128)} async-done(((f32[8192,128]{1,0:T(8,128)}), f32[512,128]{1,0:T(8,128)}) %reduce-scatter.8.cloned.1.call-update) | async-done | bytes 262160 | tf_op jit(solution)/shard_map/reduce_scatter | solution.py:51
  282.9 5.5 %fusion = f32[4,128,128,1]{2,1,3,0:T(8,128)} fusion(bf16[4,32,128,128]{3,2,1,0:T(8,128)(2,1)} %broadcast_select_fusion, bf16[4,32,128,128]{3,2,1,0:T(8,128)(2,1)} %bitcast.67, pred[4,32]{1,0:T(4,128)(4,1)S(1)} %compare_and_fusion), kind=kOutput, calls=%fused_computation.6 | convolution fusion | flops 538968064 | bytes 8650880 | tf_op jit(solution)/shard_map/rkij,rkjf->rif/dot_general | solution.py:34
  288.4 87.8 %all-reduce.3.cloned.1.call-done = (bf16[256,128]{0,1:T(8,128)(2,1)}, bf16[256,128]{1,0:T(8,128)(2,1)}) async-done(((bf16[256,128]{0,1:T(8,128)(2,1)}, bf16[256,128]{1,0:T(8,128)(2,1)}), (bf16[256,128]{0,1:T(8,128)(2,1)}, bf16[256,128]{1,0:T(8,128)(2,1)})) %all-reduce.3.cloned.1.call-update) | async-done | bytes 131088 | tf_op jit(solution)/shard_map/psum | solution.py:62
  (141 shorter events, 98.5 us)
Async XLA Ops:
  7.2 60.3 %all-gather.2.cloned.1.call-start = ((), (), s32[]{:S(2)}) async-start(), calls=%async_computation.3 | async-start | bytes 6291456 | tf_op jit(solution)/shard_map/all_gather | solution.py:66
  7.9 164.1 %reduce-scatter.4.cloned.1.call-start = ((), (), s32[]{:S(2)}) async-start(), calls=%async_computation.4 | async-start | bytes 4456448 | tf_op jit(solution)/shard_map/reduce_scatter | solution.py:51
  91.8 96.5 %reduce-scatter.6.cloned.1.call-start = ((), (), s32[]{:S(2)}) async-start(), calls=%async_computation.5 | async-start | bytes 786432 | tf_op jit(solution)/shard_map/reduce_scatter | solution.py:90
  104.1 5.4 %collective-permute-start.8 = (bf16[512,128]{0,1:T(8,128)(2,1)S(1)}, bf16[512,128]{0,1:T(8,128)(2,1)S(1)}, u32[]{:S(2)}, u32[]{:S(2)}) collective-permute-start(bf16[512,128]{0,1:T(8,128)(2,1)S(1)} %fusion.10), channel_id=1, source_target_pairs={{0,30},{2,0},{4,2},{6,4},{8,6},{10,8},{12,10},{14,12},{16,14},{18,... | collective-permute-start | bytes 393224 | tf_op jit(solution)/shard_map/ppermute | solution.py:17
  114.9 5.4 %collective-permute-start.10 = (bf16[512,128]{0,1:T(8,128)(2,1)S(1)}, bf16[512,128]{0,1:T(8,128)(2,1)S(1)}, u32[]{:S(2)}, u32[]{:S(2)}) collective-permute-start(bf16[512,128]{0,1:T(8,128)(2,1)S(1)} %collective-permute-done.9), channel_id=1, source_target_pairs={{0,30},{2,0},{4,2},{6,4},{8,6},{10,8},{12,10},{14,12},{16,14},{18,... | collective-permute-start | bytes 393224 | tf_op jit(solution)/shard_map/ppermute | solution.py:17
  120.3 7.9 %collective-permute-start.4 = (bf16[512,128]{0,1:T(8,128)(2,1)S(1)}, bf16[512,128]{0,1:T(8,128)(2,1)S(1)}, u32[]{:S(2)}, u32[]{:S(2)}) collective-permute-start(bf16[512,128]{0,1:T(8,128)(2,1)S(1)} %collective-permute-done.3), channel_id=1, source_target_pairs={{0,2},{2,4},{4,6},{6,8},{8,10},{10,12},{12,14},{14,16},{16,18},{18... | collective-permute-start | bytes 393224 | tf_op jit(solution)/shard_map/ppermute | solution.py:15
  120.3 8.2 %collective-permute-start.11 = (bf16[512,128]{0,1:T(8,128)(2,1)S(1)}, bf16[512,128]{0,1:T(8,128)(2,1)S(1)}, u32[]{:S(2)}, u32[]{:S(2)}) collective-permute-start(bf16[512,128]{0,1:T(8,128)(2,1)S(1)} %collective-permute-done.10), channel_id=1, source_target_pairs={{0,30},{2,0},{4,2},{6,4},{8,6},{10,8},{12,10},{14,12},{16,14},{18,... | collective-permute-start | bytes 393224 | tf_op jit(solution)/shard_map/ppermute | solution.py:17
  128.2 5.5 %collective-permute-start.5 = (bf16[512,128]{0,1:T(8,128)(2,1)S(1)}, bf16[512,128]{0,1:T(8,128)(2,1)S(1)}, u32[]{:S(2)}, u32[]{:S(2)}) collective-permute-start(bf16[512,128]{0,1:T(8,128)(2,1)S(1)} %collective-permute-done.4), channel_id=1, source_target_pairs={{0,2},{2,4},{4,6},{6,8},{8,10},{10,12},{12,14},{14,16},{16,18},{18... | collective-permute-start | bytes 393224 | tf_op jit(solution)/shard_map/ppermute | solution.py:15
  128.5 6.4 %collective-permute-start.12 = (bf16[512,128]{0,1:T(8,128)(2,1)S(1)}, bf16[512,128]{0,1:T(8,128)(2,1)S(1)}, u32[]{:S(2)}, u32[]{:S(2)}) collective-permute-start(bf16[512,128]{0,1:T(8,128)(2,1)S(1)} %collective-permute-done.11), channel_id=1, source_target_pairs={{0,30},{2,0},{4,2},{6,4},{8,6},{10,8},{12,10},{14,12},{16,14},{18,... | collective-permute-start | bytes 393224 | tf_op jit(solution)/shard_map/ppermute | solution.py:17
  133.7 6.0 %collective-permute-start.6 = (bf16[512,128]{0,1:T(8,128)(2,1)S(1)}, bf16[512,128]{0,1:T(8,128)(2,1)S(1)}, u32[]{:S(2)}, u32[]{:S(2)}) collective-permute-start(bf16[512,128]{0,1:T(8,128)(2,1)S(1)} %collective-permute-done.5), channel_id=1, source_target_pairs={{0,2},{2,4},{4,6},{6,8},{8,10},{10,12},{12,14},{14,16},{16,18},{18... | collective-permute-start | bytes 393224 | tf_op jit(solution)/shard_map/ppermute | solution.py:15
  134.9 6.5 %collective-permute-start.13 = (bf16[512,128]{0,1:T(8,128)(2,1)S(1)}, bf16[512,128]{0,1:T(8,128)(2,1)}, u32[]{:S(2)}, u32[]{:S(2)}) collective-permute-start(bf16[512,128]{0,1:T(8,128)(2,1)S(1)} %collective-permute-done.12), channel_id=1, source_target_pairs={{0,30},{2,0},{4,2},{6,4},{8,6},{10,8},{12,10},{14,12},{16,14},{18,... | collective-permute-start | bytes 393224 | tf_op jit(solution)/shard_map/ppermute | solution.py:17
  139.7 8.2 %collective-permute-start.7 = (bf16[512,128]{0,1:T(8,128)(2,1)S(1)}, bf16[512,128]{0,1:T(8,128)(2,1)}, u32[]{:S(2)}, u32[]{:S(2)}) collective-permute-start(bf16[512,128]{0,1:T(8,128)(2,1)S(1)} %collective-permute-done.6), channel_id=1, source_target_pairs={{0,2},{2,4},{4,6},{6,8},{8,10},{10,12},{12,14},{14,16},{16,18},{18... | collective-permute-start | bytes 393224 | tf_op jit(solution)/shard_map/ppermute | solution.py:15
  141.4 12.2 %collective-permute-start.14 = (bf16[512,128]{0,1:T(8,128)(2,1)}, bf16[512,128]{0,1:T(8,128)(2,1)S(1)}, u32[]{:S(2)}, u32[]{:S(2)}) collective-permute-start(bf16[512,128]{0,1:T(8,128)(2,1)} %collective-permute-done.13), channel_id=1, source_target_pairs={{0,30},{2,0},{4,2},{6,4},{8,6},{10,8},{12,10},{14,12},{16,14},{18,... | collective-permute-start | bytes 393224 | tf_op jit(solution)/shard_map/ppermute | solution.py:17
  174.0 107.1 %reduce-scatter.8.cloned.1.call-start = ((), (), s32[]{:S(2)}) async-start(), calls=%async_computation.6 | async-start | bytes 4456448 | tf_op jit(solution)/shard_map/reduce_scatter | solution.py:51
  201.3 174.9 %all-reduce.3.cloned.1.call-start = ((), (), s32[]{:S(2)}) async-start(), calls=%async_computation.7 | async-start | bytes 262144 | tf_op jit(solution)/shard_map/psum | solution.py:62
  212.7 5.4 %collective-permute-start.23 = (bf16[512,128]{1,0:T(8,128)(2,1)S(1)}, bf16[512,128]{1,0:T(8,128)(2,1)S(1)}, u32[]{:S(2)}, u32[]{:S(2)}) collective-permute-start(bf16[512,128]{1,0:T(8,128)(2,1)S(1)} %convolution_convert_fusion), channel_id=1, source_target_pairs={{0,30},{2,0},{4,2},{6,4},{8,6},{10,8},{12,10},{14,12},{16,14},{18,... | collective-permute-start | bytes 393224 | tf_op jit(solution)/shard_map/ppermute | solution.py:17
  228.9 8.0 %collective-permute-start.19 = (bf16[512,128]{1,0:T(8,128)(2,1)S(1)}, bf16[512,128]{1,0:T(8,128)(2,1)S(1)}, u32[]{:S(2)}, u32[]{:S(2)}) collective-permute-start(bf16[512,128]{1,0:T(8,128)(2,1)S(1)} %collective-permute-done.18), channel_id=1, source_target_pairs={{0,2},{2,4},{4,6},{6,8},{8,10},{10,12},{12,14},{14,16},{16,18},{18... | collective-permute-start | bytes 393224 | tf_op jit(solution)/shard_map/ppermute | solution.py:15
  228.9 9.0 %collective-permute-start.26 = (bf16[512,128]{1,0:T(8,128)(2,1)S(1)}, bf16[512,128]{1,0:T(8,128)(2,1)S(1)}, u32[]{:S(2)}, u32[]{:S(2)}) collective-permute-start(bf16[512,128]{1,0:T(8,128)(2,1)S(1)} %collective-permute-done.25), channel_id=1, source_target_pairs={{0,30},{2,0},{4,2},{6,4},{8,6},{10,8},{12,10},{14,12},{16,14},{18,... | collective-permute-start | bytes 393224 | tf_op jit(solution)/shard_map/ppermute | solution.py:17
  236.9 5.7 %collective-permute-start.20 = (bf16[512,128]{1,0:T(8,128)(2,1)S(1)}, bf16[512,128]{1,0:T(8,128)(2,1)S(1)}, u32[]{:S(2)}, u32[]{:S(2)}) collective-permute-start(bf16[512,128]{1,0:T(8,128)(2,1)S(1)} %collective-permute-done.19), channel_id=1, source_target_pairs={{0,2},{2,4},{4,6},{6,8},{8,10},{10,12},{12,14},{14,16},{16,18},{18... | collective-permute-start | bytes 393224 | tf_op jit(solution)/shard_map/ppermute | solution.py:15
  237.9 6.4 %collective-permute-start.27 = (bf16[512,128]{1,0:T(8,128)(2,1)S(1)}, bf16[512,128]{1,0:T(8,128)(2,1)S(1)}, u32[]{:S(2)}, u32[]{:S(2)}) collective-permute-start(bf16[512,128]{1,0:T(8,128)(2,1)S(1)} %collective-permute-done.26), channel_id=1, source_target_pairs={{0,30},{2,0},{4,2},{6,4},{8,6},{10,8},{12,10},{14,12},{16,14},{18,... | collective-permute-start | bytes 393224 | tf_op jit(solution)/shard_map/ppermute | solution.py:17
  242.6 5.7 %collective-permute-start.21 = (bf16[512,128]{1,0:T(8,128)(2,1)S(1)}, bf16[512,128]{1,0:T(8,128)(2,1)S(1)}, u32[]{:S(2)}, u32[]{:S(2)}) collective-permute-start(bf16[512,128]{1,0:T(8,128)(2,1)S(1)} %collective-permute-done.20), channel_id=1, source_target_pairs={{0,2},{2,4},{4,6},{6,8},{8,10},{10,12},{12,14},{14,16},{16,18},{18... | collective-permute-start | bytes 393224 | tf_op jit(solution)/shard_map/ppermute | solution.py:15
  244.3 5.6 %collective-permute-start.28 = (bf16[512,128]{1,0:T(8,128)(2,1)S(1)}, bf16[512,128]{1,0:T(8,128)(2,1)S(1)}, u32[]{:S(2)}, u32[]{:S(2)}) collective-permute-start(bf16[512,128]{1,0:T(8,128)(2,1)S(1)} %collective-permute-done.27), channel_id=1, source_target_pairs={{0,30},{2,0},{4,2},{6,4},{8,6},{10,8},{12,10},{14,12},{16,14},{18,... | collective-permute-start | bytes 393224 | tf_op jit(solution)/shard_map/ppermute | solution.py:17
  248.3 7.8 %collective-permute-start.22 = (bf16[512,128]{1,0:T(8,128)(2,1)S(1)}, bf16[512,128]{1,0:T(8,128)(2,1)S(1)}, u32[]{:S(2)}, u32[]{:S(2)}) collective-permute-start(bf16[512,128]{1,0:T(8,128)(2,1)S(1)} %collective-permute-done.21), channel_id=1, source_target_pairs={{0,2},{2,4},{4,6},{6,8},{8,10},{10,12},{12,14},{14,16},{16,18},{18... | collective-permute-start | bytes 393224 | tf_op jit(solution)/shard_map/ppermute | solution.py:15
  249.9 10.0 %collective-permute-start.29 = (bf16[512,128]{1,0:T(8,128)(2,1)S(1)}, bf16[512,128]{1,0:T(8,128)(2,1)S(1)}, u32[]{:S(2)}, u32[]{:S(2)}) collective-permute-start(bf16[512,128]{1,0:T(8,128)(2,1)S(1)} %collective-permute-done.28), channel_id=1, source_target_pairs={{0,30},{2,0},{4,2},{6,4},{8,6},{10,8},{12,10},{14,12},{16,14},{18,... | collective-permute-start | bytes 393224 | tf_op jit(solution)/shard_map/ppermute | solution.py:17
  (25 other events, 384.8 us)
Sparse Core Ops, SparseCore 0:
  9.5 57.8 all-gather.1
  92.0 80.0 reduce-scatter.3
  174.2 14.0 reduce-scatter.5
  201.4 79.6 reduce-scatter.7
  285.0 91.1 all-reduce.2
